TPU v7x, 512 devices: a whole 4x8x8 slice. The times are simulated.
512 devices in a mesh: row: 16 (over z, core), col: 8 (over y), layer: 4 (over x).
Axes of the slice: x: 4, y: 8, z: 8, core: 2. Of those that a mesh axis runs over, the one named last changes fastest.
Arguments:
- a_blocks: bfloat16 [4096, 128, 128], P(('row', 'col', 'layer')), may hold values from -0.5 to 0.5
- a_codes: int32 [4096], P(('row', 'col', 'layer')), may hold values from -1 to 47, as said below
- b_blocks: bfloat16 [8192, 128, 128], P(('row', 'col', 'layer')), may hold values from -6 to 6
- b_codes: int32 [8192], P(('row', 'col', 'layer')), may hold values from -1 to 23, as said below
Outputs:
- product: bfloat16 [8192, 4096], P(('row', 'layer'), 'col')
Inputs may be any that keep to these rules, and one draw needn't show every extreme that they name: `a_codes`: slots that one owner receives (same o, same r and l, all q) carry distinct codes; in every group of 8 owners some owner receives 8 live slots, and every owner at least one. `b_codes`: slots that one owner receives (same o, same c and l, all q) carry distinct codes; in every group of 16 owners some owner receives 16 live slots, and every owner at least one.
All inputs are finite; a program needn't handle non-finite values.
Results may differ from a plain program's by a relative error of at most 0.001.
Values may be sent and summed in bfloat16 or wider, within the bound.
A program may use at most 64 MiB of HBM per device.

v0:
```python
import jax
import jax.numpy as jnp
from jax import lax
from jax.sharding import PartitionSpec as P

RB = 4
CB = 4
KB = 6


def from_behind(block, axis, distance):
    devices = range(lax.axis_size(axis))
    route = [((i - distance) % len(devices), i) for i in devices]
    return lax.ppermute(block, axis, route)


def dense_left(block_stack, block_codes, part_index, pieces):
    block_width = block_stack.shape[1]
    is_live = block_codes >= 0
    row_of = block_codes // (pieces * KB)
    part_of = block_codes // KB % pieces
    inner_of = block_codes % KB
    selected = is_live & (part_of == part_index)
    row_hits = row_of[:, None] == jnp.arange(RB)[None, :]
    inner_hit = inner_of[:, None] == jnp.arange(KB)[None, :]
    weight = (selected[:, None, None] & row_hits[:, :, None] & inner_hit[:, None, :]).astype(
        jnp.bfloat16
    )
    dense_tile = jnp.einsum(
        "aik,axy->ixky", weight, block_stack, preferred_element_type=jnp.float32
    )
    return dense_tile.astype(jnp.bfloat16).reshape(RB * block_width, KB * block_width)


def dense_right(block_stack, block_codes):
    block_width = block_stack.shape[1]
    is_live = block_codes >= 0
    inner_of = block_codes // CB
    column_of = block_codes % CB
    inner_hit = inner_of[:, None] == jnp.arange(KB)[None, :]
    column_hit = column_of[:, None] == jnp.arange(CB)[None, :]
    weight = (is_live[:, None, None] & inner_hit[:, :, None] & column_hit[:, None, :]).astype(
        jnp.bfloat16
    )
    dense_tile = jnp.einsum(
        "skj,sxy->kxjy", weight, block_stack, preferred_element_type=jnp.float32
    )
    return dense_tile.astype(jnp.bfloat16).reshape(KB * block_width, CB * block_width)


def shards(a_blocks, a_codes, b_blocks, b_codes):
    row_count = lax.axis_size("row")
    col_count = lax.axis_size("col")
    pieces = row_count // col_count
    block_width = a_blocks.shape[1]
    row_index = lax.axis_index("row")
    col_index = lax.axis_index("col")
    a_stack, a_tags = (
        lax.all_to_all(a_blocks, "col", split_axis=0, concat_axis=0, tiled=True),
        lax.all_to_all(a_codes, "col", split_axis=0, concat_axis=0, tiled=True),
    )
    b_stack, b_tags = (
        lax.all_to_all(b_blocks, "row", split_axis=0, concat_axis=0, tiled=True),
        lax.all_to_all(b_codes, "row", split_axis=0, concat_axis=0, tiled=True),
    )

    def multiply(accumulated, left_stack, left_codes, right_stack, right_codes, piece_index):
        left_tile = dense_left(left_stack, left_codes, piece_index // col_count, pieces)
        right_tile = dense_right(right_stack, right_codes)
        return accumulated + jnp.dot(left_tile, right_tile, preferred_element_type=jnp.float32)

    start_sum = jnp.zeros((RB * block_width, CB * block_width), jnp.float32)

    def advance(visit_step, loop_state):
        accumulated, left_stack, left_codes, right_stack, right_codes = loop_state
        piece_index = (row_index + col_index + visit_step) % row_count
        accumulated = multiply(
            accumulated, left_stack, left_codes, right_stack, right_codes, piece_index
        )
        left_stack, left_codes = from_behind((left_stack, left_codes), "col", -1)
        right_stack, right_codes = from_behind((right_stack, right_codes), "row", -1)
        return (accumulated, left_stack, left_codes, right_stack, right_codes)

    loop_state = lax.fori_loop(
        0, row_count - 1, advance, (start_sum, a_stack, a_tags, b_stack, b_tags)
    )
    accumulated, left_stack, left_codes, right_stack, right_codes = loop_state
    last_piece = (row_index + col_index + row_count - 1) % row_count
    accumulated = multiply(
        accumulated, left_stack, left_codes, right_stack, right_codes, last_piece
    )
    reduced = lax.psum_scatter(accumulated, "layer", scatter_dimension=0, tiled=True)
    return reduced.astype(jnp.bfloat16)


def solution(mesh):
    placed = (
        P(("row", "col", "layer"), None, None),
        P(("row", "col", "layer")),
        P(("row", "col", "layer"), None, None),
        P(("row", "col", "layer")),
    )
    return jax.shard_map(
        shards, mesh=mesh, in_specs=placed, out_specs=P(("row", "layer"), "col"), check_vma=False
    )
```

profile of v0, /device:TPU:1, one launch (start us, length us, event | category | flops | bytes accessed | tf_op | source)
XLA Modules:
  0.0 346.4 jit_solution(11141364819126536148)
XLA Ops:
  7.9 7.7 %all-to-all-start.1 = ((s32[8,1,1]{2,1,0:T(1,128)}), s32[8,1,1]{2,1,0:T(1,128)S(1)}, u32[]{:S(2)}, u32[]{:S(2)}) async-start(s32[8,1,1]{2,1,0:T(1,128)} %copy.23), calls=%async_computation.1 | async-start | bytes 8192 | tf_op jit(solution)/shard_map/all_to_all | solution.py:60
  16.2 5.7 %all-to-all-done.1 = s32[8,1,1]{2,1,0:T(1,128)S(1)} async-done(((s32[8,1,1]{2,1,0:T(1,128)}), s32[8,1,1]{2,1,0:T(1,128)S(1)}, u32[]{:S(2)}, u32[]{:S(2)}) %all-to-all-start.1) | async-done | bytes 64 | tf_op jit(solution)/shard_map/all_to_all | solution.py:60
  22.0 19.2 %all_to_all.34 = s32[16,1,1]{2,1,0:T(1,128)S(1)} all-to-all(s32[16,1,1]{2,1,0:T(1,128)S(1)} %copy.24), channel_id=1, replica_groups=mesh['row'=16,'col'=8,'layer'=4] {'row'}, dimensions={0} | all-to-all | bytes 128 | tf_op jit(solution)/shard_map/all_to_all | solution.py:64
  41.2 14.3 %all_to_all.35 = bf16[8,128,128]{2,1,0:T(8,128)(2,1)S(1)} all-to-all(bf16[8,128,128]{2,1,0:T(8,128)(2,1)} %param.6), channel_id=1, replica_groups=mesh['row'=16,'col'=8,'layer'=4] {'col'}, dimensions={0} | all-to-all | bytes 524288 | tf_op jit(solution)/shard_map/all_to_all | solution.py:59
  55.5 5.2 %all-to-all-start.2 = ((bf16[16,128,128]{2,1,0:T(8,128)(2,1)}), bf16[16,128,128]{2,1,0:T(8,128)(2,1)S(1)}, u32[]{:S(2)}, u32[]{:S(2)}) async-start(bf16[16,128,128]{2,1,0:T(8,128)(2,1)} %param.8), calls=%async_computation.2 | async-start | bytes 1048576 | tf_op jit(solution)/shard_map/all_to_all | solution.py:63
  61.6 16.5 %all-to-all-done.2 = bf16[16,128,128]{2,1,0:T(8,128)(2,1)S(1)} async-done(((bf16[16,128,128]{2,1,0:T(8,128)(2,1)}), bf16[16,128,128]{2,1,0:T(8,128)(2,1)S(1)}, u32[]{:S(2)}, u32[]{:S(2)}) %all-to-all-start.2) | async-done | bytes 524320 | tf_op jit(solution)/shard_map/all_to_all | solution.py:63
  78.4 224.5 %while.25 = (s32[]{:T(128)}, f32[512,512]{1,0:T(8,128)S(1)}, bf16[8,128,128]{2,0,1:T(8,128)(2,1)S(1)}, s32[8]{0:T(128)S(1)}, bf16[16,128,128]{2,0,1:T(8,128)(2,1...) while((s32[]{:T(128)}, f32[512,512]{1,0:T(8,128)S(1)}, ...), condition=%wide.region_1.2_spmd.clone, body=%wide.region_0.1_spmd.clone.sunk | while | flops 422839840 | bytes 12323026 | solution.py:84
  87.7 3.7 %collective-permute-done.3 = s32[16]{0:T(128)S(1)} collective-permute-done((s32[16]{0:T(128)S(1)}, s32[16]{0:T(128)S(1)}, u32[]{:S(2)}, u32[]{:S(2)}) %collective-permute-start.3) | collective-permute-done | bytes 96 | tf_op jit(solution)/shard_map/while/body/eval_jaxpr/ppermute | solution.py:14
  99.3 5.5 %collective-permute-done.3 = s32[16]{0:T(128)S(1)} collective-permute-done((s32[16]{0:T(128)S(1)}, s32[16]{0:T(128)S(1)}, u32[]{:S(2)}, u32[]{:S(2)}) %collective-permute-start.3) | collective-permute-done | bytes 96 | tf_op jit(solution)/shard_map/while/body/eval_jaxpr/ppermute | solution.py:14
  104.8 4.0 %collective-permute-start = (bf16[8,128,128]{2,0,1:T(8,128)(2,1)S(1)}, bf16[8,128,128]{2,0,1:T(8,128)(2,1)S(1)}, u32[]{:S(2)}, u32[]{:S(2)}) collective-permute-start(bf16[8,128,128]{2,0,1:T(8,128)(2,1)S(1)} %copy.68), channel_id=1, source_target_pairs={{4,0},{8,4},{12,8},{16,12},{20,16},{24,20},{28,24},{0,28},{5,1},{9... | collective-permute-start | bytes 786440 | tf_op jit(solution)/shard_map/while/body/eval_jaxpr/ppermute | solution.py:14
  115.5 4.7 %collective-permute-done.3 = s32[16]{0:T(128)S(1)} collective-permute-done((s32[16]{0:T(128)S(1)}, s32[16]{0:T(128)S(1)}, u32[]{:S(2)}, u32[]{:S(2)}) %collective-permute-start.3) | collective-permute-done | bytes 96 | tf_op jit(solution)/shard_map/while/body/eval_jaxpr/ppermute | solution.py:14
  120.2 3.8 %collective-permute-start = (bf16[8,128,128]{2,0,1:T(8,128)(2,1)S(1)}, bf16[8,128,128]{2,0,1:T(8,128)(2,1)S(1)}, u32[]{:S(2)}, u32[]{:S(2)}) collective-permute-start(bf16[8,128,128]{2,0,1:T(8,128)(2,1)S(1)} %copy.68), channel_id=1, source_target_pairs={{4,0},{8,4},{12,8},{16,12},{20,16},{24,20},{28,24},{0,28},{5,1},{9... | collective-permute-start | bytes 786440 | tf_op jit(solution)/shard_map/while/body/eval_jaxpr/ppermute | solution.py:14
  124.0 3.1 collective-permute-start.1
  132.4 3.5 collective-permute-done.3
  153.5 2.8 collective-permute-start.2
  162.2 4.0 %collective-permute-start = (bf16[8,128,128]{2,0,1:T(8,128)(2,1)S(1)}, bf16[8,128,128]{2,0,1:T(8,128)(2,1)S(1)}, u32[]{:S(2)}, u32[]{:S(2)}) collective-permute-start(bf16[8,128,128]{2,0,1:T(8,128)(2,1)S(1)} %copy.68), channel_id=1, source_target_pairs={{4,0},{8,4},{12,8},{16,12},{20,16},{24,20},{28,24},{0,28},{5,1},{9... | collective-permute-start | bytes 786440 | tf_op jit(solution)/shard_map/while/body/eval_jaxpr/ppermute | solution.py:14
  169.0 4.0 %collective-permute-start.2 = (bf16[16,128,128]{2,0,1:T(8,128)(2,1)S(1)}, bf16[16,128,128]{2,0,1:T(8,128)(2,1)S(1)}, u32[]{:S(2)}, u32[]{:S(2)}) collective-permute-start(bf16[16,128,128]{2,0,1:T(8,128)(2,1)S(1)} %copy.70), channel_id=1, source_target_pairs={{32,0},{64,32},{96,64},{128,96},{160,128},{192,160},{224,192},{256... | collective-permute-start | bytes 1572872 | tf_op jit(solution)/shard_map/while/body/eval_jaxpr/ppermute | solution.py:14
  177.9 3.8 %collective-permute-start = (bf16[8,128,128]{2,0,1:T(8,128)(2,1)S(1)}, bf16[8,128,128]{2,0,1:T(8,128)(2,1)S(1)}, u32[]{:S(2)}, u32[]{:S(2)}) collective-permute-start(bf16[8,128,128]{2,0,1:T(8,128)(2,1)S(1)} %copy.68), channel_id=1, source_target_pairs={{4,0},{8,4},{12,8},{16,12},{20,16},{24,20},{28,24},{0,28},{5,1},{9... | collective-permute-start | bytes 786440 | tf_op jit(solution)/shard_map/while/body/eval_jaxpr/ppermute | solution.py:14
  181.7 3.1 collective-permute-start.1
  184.9 5.0 %collective-permute-start.2 = (bf16[16,128,128]{2,0,1:T(8,128)(2,1)S(1)}, bf16[16,128,128]{2,0,1:T(8,128)(2,1)S(1)}, u32[]{:S(2)}, u32[]{:S(2)}) collective-permute-start(bf16[16,128,128]{2,0,1:T(8,128)(2,1)S(1)} %copy.70), channel_id=1, source_target_pairs={{32,0},{64,32},{96,64},{128,96},{160,128},{192,160},{224,192},{256... | collective-permute-start | bytes 1572872 | tf_op jit(solution)/shard_map/while/body/eval_jaxpr/ppermute | solution.py:14
  199.0 5.0 %collective-permute-start.2 = (bf16[16,128,128]{2,0,1:T(8,128)(2,1)S(1)}, bf16[16,128,128]{2,0,1:T(8,128)(2,1)S(1)}, u32[]{:S(2)}, u32[]{:S(2)}) collective-permute-start(bf16[16,128,128]{2,0,1:T(8,128)(2,1)S(1)} %copy.70), channel_id=1, source_target_pairs={{32,0},{64,32},{96,64},{128,96},{160,128},{192,160},{224,192},{256... | collective-permute-start | bytes 1572872 | tf_op jit(solution)/shard_map/while/body/eval_jaxpr/ppermute | solution.py:14
  213.6 5.0 %collective-permute-start.2 = (bf16[16,128,128]{2,0,1:T(8,128)(2,1)S(1)}, bf16[16,128,128]{2,0,1:T(8,128)(2,1)S(1)}, u32[]{:S(2)}, u32[]{:S(2)}) collective-permute-start(bf16[16,128,128]{2,0,1:T(8,128)(2,1)S(1)} %copy.70), channel_id=1, source_target_pairs={{32,0},{64,32},{96,64},{128,96},{160,128},{192,160},{224,192},{256... | collective-permute-start | bytes 1572872 | tf_op jit(solution)/shard_map/while/body/eval_jaxpr/ppermute | solution.py:14
  223.7 4.2 %collective-permute-start = (bf16[8,128,128]{2,0,1:T(8,128)(2,1)S(1)}, bf16[8,128,128]{2,0,1:T(8,128)(2,1)S(1)}, u32[]{:S(2)}, u32[]{:S(2)}) collective-permute-start(bf16[8,128,128]{2,0,1:T(8,128)(2,1)S(1)} %copy.68), channel_id=1, source_target_pairs={{4,0},{8,4},{12,8},{16,12},{20,16},{24,20},{28,24},{0,28},{5,1},{9... | collective-permute-start | bytes 786440 | tf_op jit(solution)/shard_map/while/body/eval_jaxpr/ppermute | solution.py:14
  230.3 5.0 %collective-permute-start.2 = (bf16[16,128,128]{2,0,1:T(8,128)(2,1)S(1)}, bf16[16,128,128]{2,0,1:T(8,128)(2,1)S(1)}, u32[]{:S(2)}, u32[]{:S(2)}) collective-permute-start(bf16[16,128,128]{2,0,1:T(8,128)(2,1)S(1)} %copy.70), channel_id=1, source_target_pairs={{32,0},{64,32},{96,64},{128,96},{160,128},{192,160},{224,192},{256... | collective-permute-start | bytes 1572872 | tf_op jit(solution)/shard_map/while/body/eval_jaxpr/ppermute | solution.py:14
  240.2 4.3 %collective-permute-start = (bf16[8,128,128]{2,0,1:T(8,128)(2,1)S(1)}, bf16[8,128,128]{2,0,1:T(8,128)(2,1)S(1)}, u32[]{:S(2)}, u32[]{:S(2)}) collective-permute-start(bf16[8,128,128]{2,0,1:T(8,128)(2,1)S(1)} %copy.68), channel_id=1, source_target_pairs={{4,0},{8,4},{12,8},{16,12},{20,16},{24,20},{28,24},{0,28},{5,1},{9... | collective-permute-start | bytes 786440 | tf_op jit(solution)/shard_map/while/body/eval_jaxpr/ppermute | solution.py:14
  247.2 5.0 %collective-permute-start.2 = (bf16[16,128,128]{2,0,1:T(8,128)(2,1)S(1)}, bf16[16,128,128]{2,0,1:T(8,128)(2,1)S(1)}, u32[]{:S(2)}, u32[]{:S(2)}) collective-permute-start(bf16[16,128,128]{2,0,1:T(8,128)(2,1)S(1)} %copy.70), channel_id=1, source_target_pairs={{32,0},{64,32},{96,64},{128,96},{160,128},{192,160},{224,192},{256... | collective-permute-start | bytes 1572872 | tf_op jit(solution)/shard_map/while/body/eval_jaxpr/ppermute | solution.py:14
  261.7 5.0 %collective-permute-start.2 = (bf16[16,128,128]{2,0,1:T(8,128)(2,1)S(1)}, bf16[16,128,128]{2,0,1:T(8,128)(2,1)S(1)}, u32[]{:S(2)}, u32[]{:S(2)}) collective-permute-start(bf16[16,128,128]{2,0,1:T(8,128)(2,1)S(1)} %copy.70), channel_id=1, source_target_pairs={{32,0},{64,32},{96,64},{128,96},{160,128},{192,160},{224,192},{256... | collective-permute-start | bytes 1572872 | tf_op jit(solution)/shard_map/while/body/eval_jaxpr/ppermute | solution.py:14
  266.7 2.8 collective-permute-start.3
  276.3 5.0 %collective-permute-start.2 = (bf16[16,128,128]{2,0,1:T(8,128)(2,1)S(1)}, bf16[16,128,128]{2,0,1:T(8,128)(2,1)S(1)}, u32[]{:S(2)}, u32[]{:S(2)}) collective-permute-start(bf16[16,128,128]{2,0,1:T(8,128)(2,1)S(1)} %copy.70), channel_id=1, source_target_pairs={{32,0},{64,32},{96,64},{128,96},{160,128},{192,160},{224,192},{256... | collective-permute-start | bytes 1572872 | tf_op jit(solution)/shard_map/while/body/eval_jaxpr/ppermute | solution.py:14
  286.5 4.2 %collective-permute-start = (bf16[8,128,128]{2,0,1:T(8,128)(2,1)S(1)}, bf16[8,128,128]{2,0,1:T(8,128)(2,1)S(1)}, u32[]{:S(2)}, u32[]{:S(2)}) collective-permute-start(bf16[8,128,128]{2,0,1:T(8,128)(2,1)S(1)} %copy.68), channel_id=1, source_target_pairs={{4,0},{8,4},{12,8},{16,12},{20,16},{24,20},{28,24},{0,28},{5,1},{9... | collective-permute-start | bytes 786440 | tf_op jit(solution)/shard_map/while/body/eval_jaxpr/ppermute | solution.py:14
  292.7 5.0 %collective-permute-start.2 = (bf16[16,128,128]{2,0,1:T(8,128)(2,1)S(1)}, bf16[16,128,128]{2,0,1:T(8,128)(2,1)S(1)}, u32[]{:S(2)}, u32[]{:S(2)}) collective-permute-start(bf16[16,128,128]{2,0,1:T(8,128)(2,1)S(1)} %copy.70), channel_id=1, source_target_pairs={{32,0},{64,32},{96,64},{128,96},{160,128},{192,160},{224,192},{256... | collective-permute-start | bytes 1572872 | tf_op jit(solution)/shard_map/while/body/eval_jaxpr/ppermute | solution.py:14
  308.7 29.2 %reduce-scatter.2.cloned.1.call-done = f32[128,512]{1,0:T(8,128)} async-done(((f32[512,512]{1,0:T(8,128)}), f32[128,512]{1,0:T(8,128)}) %reduce-scatter.2.cloned.1.call-update) | async-done | bytes 262160 | tf_op jit(solution)/shard_map/reduce_scatter | solution.py:92
  (359 shorter events, 130.5 us)
Async XLA Ops:
  7.9 14.1 %all-to-all-start.1 = ((s32[8,1,1]{2,1,0:T(1,128)}), s32[8,1,1]{2,1,0:T(1,128)S(1)}, u32[]{:S(2)}, u32[]{:S(2)}) async-start(s32[8,1,1]{2,1,0:T(1,128)} %copy.23), calls=%async_computation.1 | async-start | bytes 8192 | tf_op jit(solution)/shard_map/all_to_all | solution.py:60
  55.5 22.5 %all-to-all-start.2 = ((bf16[16,128,128]{2,1,0:T(8,128)(2,1)}), bf16[16,128,128]{2,1,0:T(8,128)(2,1)S(1)}, u32[]{:S(2)}, u32[]{:S(2)}) async-start(bf16[16,128,128]{2,1,0:T(8,128)(2,1)} %param.8), calls=%async_computation.2 | async-start | bytes 1048576 | tf_op jit(solution)/shard_map/all_to_all | solution.py:63
  60.7 277.2 %reduce-scatter.2.cloned.1.call-start = ((), (), s32[]{:S(2)}) async-start(), calls=%async_computation.5 | async-start | bytes 1310720 | tf_op jit(solution)/shard_map/reduce_scatter | solution.py:92
  78.4 12.9 %collective-permute-start = (bf16[8,128,128]{2,0,1:T(8,128)(2,1)S(1)}, bf16[8,128,128]{2,0,1:T(8,128)(2,1)S(1)}, u32[]{:S(2)}, u32[]{:S(2)}) collective-permute-start(bf16[8,128,128]{2,0,1:T(8,128)(2,1)S(1)} %copy.68), channel_id=1, source_target_pairs={{4,0},{8,4},{12,8},{16,12},{20,16},{24,20},{28,24},{0,28},{5,1},{9... | collective-permute-start | bytes 786440 | tf_op jit(solution)/shard_map/while/body/eval_jaxpr/ppermute | solution.py:14
  91.4 13.3 %collective-permute-start = (bf16[8,128,128]{2,0,1:T(8,128)(2,1)S(1)}, bf16[8,128,128]{2,0,1:T(8,128)(2,1)S(1)}, u32[]{:S(2)}, u32[]{:S(2)}) collective-permute-start(bf16[8,128,128]{2,0,1:T(8,128)(2,1)S(1)} %copy.68), channel_id=1, source_target_pairs={{4,0},{8,4},{12,8},{16,12},{20,16},{24,20},{28,24},{0,28},{5,1},{9... | collective-permute-start | bytes 786440 | tf_op jit(solution)/shard_map/while/body/eval_jaxpr/ppermute | solution.py:14
  104.8 15.5 %collective-permute-start = (bf16[8,128,128]{2,0,1:T(8,128)(2,1)S(1)}, bf16[8,128,128]{2,0,1:T(8,128)(2,1)S(1)}, u32[]{:S(2)}, u32[]{:S(2)}) collective-permute-start(bf16[8,128,128]{2,0,1:T(8,128)(2,1)S(1)} %copy.68), channel_id=1, source_target_pairs={{4,0},{8,4},{12,8},{16,12},{20,16},{24,20},{28,24},{0,28},{5,1},{9... | collective-permute-start | bytes 786440 | tf_op jit(solution)/shard_map/while/body/eval_jaxpr/ppermute | solution.py:14
  120.2 15.6 %collective-permute-start = (bf16[8,128,128]{2,0,1:T(8,128)(2,1)S(1)}, bf16[8,128,128]{2,0,1:T(8,128)(2,1)S(1)}, u32[]{:S(2)}, u32[]{:S(2)}) collective-permute-start(bf16[8,128,128]{2,0,1:T(8,128)(2,1)S(1)} %copy.68), channel_id=1, source_target_pairs={{4,0},{8,4},{12,8},{16,12},{20,16},{24,20},{28,24},{0,28},{5,1},{9... | collective-permute-start | bytes 786440 | tf_op jit(solution)/shard_map/while/body/eval_jaxpr/ppermute | solution.py:14
  135.9 13.0 %collective-permute-start = (bf16[8,128,128]{2,0,1:T(8,128)(2,1)S(1)}, bf16[8,128,128]{2,0,1:T(8,128)(2,1)S(1)}, u32[]{:S(2)}, u32[]{:S(2)}) collective-permute-start(bf16[8,128,128]{2,0,1:T(8,128)(2,1)S(1)} %copy.68), channel_id=1, source_target_pairs={{4,0},{8,4},{12,8},{16,12},{20,16},{24,20},{28,24},{0,28},{5,1},{9... | collective-permute-start | bytes 786440 | tf_op jit(solution)/shard_map/while/body/eval_jaxpr/ppermute | solution.py:14
  148.9 13.3 %collective-permute-start = (bf16[8,128,128]{2,0,1:T(8,128)(2,1)S(1)}, bf16[8,128,128]{2,0,1:T(8,128)(2,1)S(1)}, u32[]{:S(2)}, u32[]{:S(2)}) collective-permute-start(bf16[8,128,128]{2,0,1:T(8,128)(2,1)S(1)} %copy.68), channel_id=1, source_target_pairs={{4,0},{8,4},{12,8},{16,12},{20,16},{24,20},{28,24},{0,28},{5,1},{9... | collective-permute-start | bytes 786440 | tf_op jit(solution)/shard_map/while/body/eval_jaxpr/ppermute | solution.py:14
  162.2 15.6 %collective-permute-start = (bf16[8,128,128]{2,0,1:T(8,128)(2,1)S(1)}, bf16[8,128,128]{2,0,1:T(8,128)(2,1)S(1)}, u32[]{:S(2)}, u32[]{:S(2)}) collective-permute-start(bf16[8,128,128]{2,0,1:T(8,128)(2,1)S(1)} %copy.68), channel_id=1, source_target_pairs={{4,0},{8,4},{12,8},{16,12},{20,16},{24,20},{28,24},{0,28},{5,1},{9... | collective-permute-start | bytes 786440 | tf_op jit(solution)/shard_map/while/body/eval_jaxpr/ppermute | solution.py:14
  166.2 11.6 %collective-permute-start.1 = (s32[8]{0:T(128)S(1)}, s32[8]{0:T(128)S(1)}, u32[]{:S(2)}, u32[]{:S(2)}) collective-permute-start(s32[8]{0:T(128)S(1)} %copy.69), channel_id=1, source_target_pairs={{4,0},{8,4},{12,8},{16,12},{20,16},{24,20},{28,24},{0,28},{5,1},{9... | collective-permute-start | bytes 104 | tf_op jit(solution)/shard_map/while/body/eval_jaxpr/ppermute | solution.py:14
  177.9 16.8 %collective-permute-start = (bf16[8,128,128]{2,0,1:T(8,128)(2,1)S(1)}, bf16[8,128,128]{2,0,1:T(8,128)(2,1)S(1)}, u32[]{:S(2)}, u32[]{:S(2)}) collective-permute-start(bf16[8,128,128]{2,0,1:T(8,128)(2,1)S(1)} %copy.68), channel_id=1, source_target_pairs={{4,0},{8,4},{12,8},{16,12},{20,16},{24,20},{28,24},{0,28},{5,1},{9... | collective-permute-start | bytes 786440 | tf_op jit(solution)/shard_map/while/body/eval_jaxpr/ppermute | solution.py:14
  181.7 13.0 %collective-permute-start.1 = (s32[8]{0:T(128)S(1)}, s32[8]{0:T(128)S(1)}, u32[]{:S(2)}, u32[]{:S(2)}) collective-permute-start(s32[8]{0:T(128)S(1)} %copy.69), channel_id=1, source_target_pairs={{4,0},{8,4},{12,8},{16,12},{20,16},{24,20},{28,24},{0,28},{5,1},{9... | collective-permute-start | bytes 104 | tf_op jit(solution)/shard_map/while/body/eval_jaxpr/ppermute | solution.py:14
  194.8 14.2 %collective-permute-start = (bf16[8,128,128]{2,0,1:T(8,128)(2,1)S(1)}, bf16[8,128,128]{2,0,1:T(8,128)(2,1)S(1)}, u32[]{:S(2)}, u32[]{:S(2)}) collective-permute-start(bf16[8,128,128]{2,0,1:T(8,128)(2,1)S(1)} %copy.68), channel_id=1, source_target_pairs={{4,0},{8,4},{12,8},{16,12},{20,16},{24,20},{28,24},{0,28},{5,1},{9... | collective-permute-start | bytes 786440 | tf_op jit(solution)/shard_map/while/body/eval_jaxpr/ppermute | solution.py:14
  197.0 12.0 %collective-permute-start.1 = (s32[8]{0:T(128)S(1)}, s32[8]{0:T(128)S(1)}, u32[]{:S(2)}, u32[]{:S(2)}) collective-permute-start(s32[8]{0:T(128)S(1)} %copy.69), channel_id=1, source_target_pairs={{4,0},{8,4},{12,8},{16,12},{20,16},{24,20},{28,24},{0,28},{5,1},{9... | collective-permute-start | bytes 104 | tf_op jit(solution)/shard_map/while/body/eval_jaxpr/ppermute | solution.py:14
  199.0 10.0 %collective-permute-start.2 = (bf16[16,128,128]{2,0,1:T(8,128)(2,1)S(1)}, bf16[16,128,128]{2,0,1:T(8,128)(2,1)S(1)}, u32[]{:S(2)}, u32[]{:S(2)}) collective-permute-start(bf16[16,128,128]{2,0,1:T(8,128)(2,1)S(1)} %copy.70), channel_id=1, source_target_pairs={{32,0},{64,32},{96,64},{128,96},{160,128},{192,160},{224,192},{256... | collective-permute-start | bytes 1572872 | tf_op jit(solution)/shard_map/while/body/eval_jaxpr/ppermute | solution.py:14
  209.1 14.6 %collective-permute-start = (bf16[8,128,128]{2,0,1:T(8,128)(2,1)S(1)}, bf16[8,128,128]{2,0,1:T(8,128)(2,1)S(1)}, u32[]{:S(2)}, u32[]{:S(2)}) collective-permute-start(bf16[8,128,128]{2,0,1:T(8,128)(2,1)S(1)} %copy.68), channel_id=1, source_target_pairs={{4,0},{8,4},{12,8},{16,12},{20,16},{24,20},{28,24},{0,28},{5,1},{9... | collective-permute-start | bytes 786440 | tf_op jit(solution)/shard_map/while/body/eval_jaxpr/ppermute | solution.py:14
  211.6 12.0 %collective-permute-start.1 = (s32[8]{0:T(128)S(1)}, s32[8]{0:T(128)S(1)}, u32[]{:S(2)}, u32[]{:S(2)}) collective-permute-start(s32[8]{0:T(128)S(1)} %copy.69), channel_id=1, source_target_pairs={{4,0},{8,4},{12,8},{16,12},{20,16},{24,20},{28,24},{0,28},{5,1},{9... | collective-permute-start | bytes 104 | tf_op jit(solution)/shard_map/while/body/eval_jaxpr/ppermute | solution.py:14
  213.6 10.1 %collective-permute-start.2 = (bf16[16,128,128]{2,0,1:T(8,128)(2,1)S(1)}, bf16[16,128,128]{2,0,1:T(8,128)(2,1)S(1)}, u32[]{:S(2)}, u32[]{:S(2)}) collective-permute-start(bf16[16,128,128]{2,0,1:T(8,128)(2,1)S(1)} %copy.70), channel_id=1, source_target_pairs={{32,0},{64,32},{96,64},{128,96},{160,128},{192,160},{224,192},{256... | collective-permute-start | bytes 1572872 | tf_op jit(solution)/shard_map/while/body/eval_jaxpr/ppermute | solution.py:14
  223.7 16.4 %collective-permute-start = (bf16[8,128,128]{2,0,1:T(8,128)(2,1)S(1)}, bf16[8,128,128]{2,0,1:T(8,128)(2,1)S(1)}, u32[]{:S(2)}, u32[]{:S(2)}) collective-permute-start(bf16[8,128,128]{2,0,1:T(8,128)(2,1)S(1)} %copy.68), channel_id=1, source_target_pairs={{4,0},{8,4},{12,8},{16,12},{20,16},{24,20},{28,24},{0,28},{5,1},{9... | collective-permute-start | bytes 786440 | tf_op jit(solution)/shard_map/while/body/eval_jaxpr/ppermute | solution.py:14
  228.0 12.2 %collective-permute-start.1 = (s32[8]{0:T(128)S(1)}, s32[8]{0:T(128)S(1)}, u32[]{:S(2)}, u32[]{:S(2)}) collective-permute-start(s32[8]{0:T(128)S(1)} %copy.69), channel_id=1, source_target_pairs={{4,0},{8,4},{12,8},{16,12},{20,16},{24,20},{28,24},{0,28},{5,1},{9... | collective-permute-start | bytes 104 | tf_op jit(solution)/shard_map/while/body/eval_jaxpr/ppermute | solution.py:14
  240.2 16.8 %collective-permute-start = (bf16[8,128,128]{2,0,1:T(8,128)(2,1)S(1)}, bf16[8,128,128]{2,0,1:T(8,128)(2,1)S(1)}, u32[]{:S(2)}, u32[]{:S(2)}) collective-permute-start(bf16[8,128,128]{2,0,1:T(8,128)(2,1)S(1)} %copy.68), channel_id=1, source_target_pairs={{4,0},{8,4},{12,8},{16,12},{20,16},{24,20},{28,24},{0,28},{5,1},{9... | collective-permute-start | bytes 786440 | tf_op jit(solution)/shard_map/while/body/eval_jaxpr/ppermute | solution.py:14
  244.5 12.5 %collective-permute-start.1 = (s32[8]{0:T(128)S(1)}, s32[8]{0:T(128)S(1)}, u32[]{:S(2)}, u32[]{:S(2)}) collective-permute-start(s32[8]{0:T(128)S(1)} %copy.69), channel_id=1, source_target_pairs={{4,0},{8,4},{12,8},{16,12},{20,16},{24,20},{28,24},{0,28},{5,1},{9... | collective-permute-start | bytes 104 | tf_op jit(solution)/shard_map/while/body/eval_jaxpr/ppermute | solution.py:14
  257.1 14.7 %collective-permute-start = (bf16[8,128,128]{2,0,1:T(8,128)(2,1)S(1)}, bf16[8,128,128]{2,0,1:T(8,128)(2,1)S(1)}, u32[]{:S(2)}, u32[]{:S(2)}) collective-permute-start(bf16[8,128,128]{2,0,1:T(8,128)(2,1)S(1)} %copy.68), channel_id=1, source_target_pairs={{4,0},{8,4},{12,8},{16,12},{20,16},{24,20},{28,24},{0,28},{5,1},{9... | collective-permute-start | bytes 786440 | tf_op jit(solution)/shard_map/while/body/eval_jaxpr/ppermute | solution.py:14
  259.7 12.0 %collective-permute-start.1 = (s32[8]{0:T(128)S(1)}, s32[8]{0:T(128)S(1)}, u32[]{:S(2)}, u32[]{:S(2)}) collective-permute-start(s32[8]{0:T(128)S(1)} %copy.69), channel_id=1, source_target_pairs={{4,0},{8,4},{12,8},{16,12},{20,16},{24,20},{28,24},{0,28},{5,1},{9... | collective-permute-start | bytes 104 | tf_op jit(solution)/shard_map/while/body/eval_jaxpr/ppermute | solution.py:14
  261.7 10.1 %collective-permute-start.2 = (bf16[16,128,128]{2,0,1:T(8,128)(2,1)S(1)}, bf16[16,128,128]{2,0,1:T(8,128)(2,1)S(1)}, u32[]{:S(2)}, u32[]{:S(2)}) collective-permute-start(bf16[16,128,128]{2,0,1:T(8,128)(2,1)S(1)} %copy.70), channel_id=1, source_target_pairs={{32,0},{64,32},{96,64},{128,96},{160,128},{192,160},{224,192},{256... | collective-permute-start | bytes 1572872 | tf_op jit(solution)/shard_map/while/body/eval_jaxpr/ppermute | solution.py:14
  271.9 14.6 %collective-permute-start = (bf16[8,128,128]{2,0,1:T(8,128)(2,1)S(1)}, bf16[8,128,128]{2,0,1:T(8,128)(2,1)S(1)}, u32[]{:S(2)}, u32[]{:S(2)}) collective-permute-start(bf16[8,128,128]{2,0,1:T(8,128)(2,1)S(1)} %copy.68), channel_id=1, source_target_pairs={{4,0},{8,4},{12,8},{16,12},{20,16},{24,20},{28,24},{0,28},{5,1},{9... | collective-permute-start | bytes 786440 | tf_op jit(solution)/shard_map/while/body/eval_jaxpr/ppermute | solution.py:14
  274.4 12.0 %collective-permute-start.1 = (s32[8]{0:T(128)S(1)}, s32[8]{0:T(128)S(1)}, u32[]{:S(2)}, u32[]{:S(2)}) collective-permute-start(s32[8]{0:T(128)S(1)} %copy.69), channel_id=1, source_target_pairs={{4,0},{8,4},{12,8},{16,12},{20,16},{24,20},{28,24},{0,28},{5,1},{9... | collective-permute-start | bytes 104 | tf_op jit(solution)/shard_map/while/body/eval_jaxpr/ppermute | solution.py:14
  276.3 10.1 %collective-permute-start.2 = (bf16[16,128,128]{2,0,1:T(8,128)(2,1)S(1)}, bf16[16,128,128]{2,0,1:T(8,128)(2,1)S(1)}, u32[]{:S(2)}, u32[]{:S(2)}) collective-permute-start(bf16[16,128,128]{2,0,1:T(8,128)(2,1)S(1)} %copy.70), channel_id=1, source_target_pairs={{32,0},{64,32},{96,64},{128,96},{160,128},{192,160},{224,192},{256... | collective-permute-start | bytes 1572872 | tf_op jit(solution)/shard_map/while/body/eval_jaxpr/ppermute | solution.py:14
  286.5 16.3 %collective-permute-start = (bf16[8,128,128]{2,0,1:T(8,128)(2,1)S(1)}, bf16[8,128,128]{2,0,1:T(8,128)(2,1)S(1)}, u32[]{:S(2)}, u32[]{:S(2)}) collective-permute-start(bf16[8,128,128]{2,0,1:T(8,128)(2,1)S(1)} %copy.68), channel_id=1, source_target_pairs={{4,0},{8,4},{12,8},{16,12},{20,16},{24,20},{28,24},{0,28},{5,1},{9... | collective-permute-start | bytes 786440 | tf_op jit(solution)/shard_map/while/body/eval_jaxpr/ppermute | solution.py:14
  290.8 12.0 %collective-permute-start.1 = (s32[8]{0:T(128)S(1)}, s32[8]{0:T(128)S(1)}, u32[]{:S(2)}, u32[]{:S(2)}) collective-permute-start(s32[8]{0:T(128)S(1)} %copy.69), channel_id=1, source_target_pairs={{4,0},{8,4},{12,8},{16,12},{20,16},{24,20},{28,24},{0,28},{5,1},{9... | collective-permute-start | bytes 104 | tf_op jit(solution)/shard_map/while/body/eval_jaxpr/ppermute | solution.py:14
  292.7 10.1 %collective-permute-start.2 = (bf16[16,128,128]{2,0,1:T(8,128)(2,1)S(1)}, bf16[16,128,128]{2,0,1:T(8,128)(2,1)S(1)}, u32[]{:S(2)}, u32[]{:S(2)}) collective-permute-start(bf16[16,128,128]{2,0,1:T(8,128)(2,1)S(1)} %copy.70), channel_id=1, source_target_pairs={{32,0},{64,32},{96,64},{128,96},{160,128},{192,160},{224,192},{256... | collective-permute-start | bytes 1572872 | tf_op jit(solution)/shard_map/while/body/eval_jaxpr/ppermute | solution.py:14
  (31 other events, 228.6 us)
Sparse Core Ops, SparseCore 0:
  308.9 29.0 reduce-scatter.1
where the time goes:
time: 349 us; the launch traced here: 346 us
  starting transfers between devices  178 us (51%)
  waiting for transfers between devices  75.2 us (22%)
  blocking collectives  33.6 us (10%)
  matrix products  24.6 us (7%)
  local copies, waits for them, and re-layouts  14.8 us (4%)
  between operations  13.5 us (4%)
  other arithmetic  3.58 us (1%)
    ppermute x60, starting transfers between devices, from_behind(): return lax.ppermute(block, axis, route)  165 us
    reduce_scatter x1, waiting for transfers between devices, shards(): lax.psum_scatter(accumulated, 'layer', scatter_dimension=0, tiled=True)  29.2 us
    ppermute x60, waiting for transfers between devices, from_behind(): return lax.ppermute(block, axis, route)  23.9 us
    all_to_all x1, blocking collectives, shards(): lax.all_to_all(b_codes, 'row', split_axis=0, concat_axis=0, tiled=True)  19.2 us
    all_to_all x1, waiting for transfers between devices, shards(): lax.all_to_all(b_blocks, 'row', split_axis=0, concat_axis=0, tiled=True)  16.5 us
    all_to_all x1, blocking collectives, shards(): lax.all_to_all(a_blocks, 'col', split_axis=0, concat_axis=0, tiled=True)  14.3 us
    dot_general x16, matrix products, multiply(): jnp.dot(left_tile, right_tile, preferred_element_type=jnp.float32)  13.2 us
    convert_element_type x16, local copies, waits for them, and re-layouts, dense_right(): dense_tile.astype(jnp.bfloat16).reshape(KB * block_width, CB * block_width)  9.46 us
  transfers between devices with their start and end apart: 63, of which 11 were waited for; matrix products, arithmetic and copies ran while one was open for 10% of the time, Pallas kernels for 0%

commit v1 on v0

v1 whole, which is shorter than its diff:
```python
import functools

import jax
import jax.numpy as jnp
from jax import lax
from jax.experimental import pallas as pl
from jax.experimental.pallas import tpu as pltpu
from jax.sharding import PartitionSpec as P

RB = 4
CB = 4
KB = 6
LANES = 128
MESH = pl.DeviceIdType.MESH


def kernel(
    rows, cols, pieces,
    a_codes, b_codes, a_in, b_in, out,
    a_all, a_tags, b_tags, table, table_s, left, right, total, passing, arrived,
    a_send, a_recv, at_send, at_recv, b_send, b_recv, p_send, p_recv,
    bt_send, bt_recv, pt_send, pt_recv, here, table_sem, x_send, x_recv,
    *b_all,
):
    chips = rows // 2
    row = lax.axis_index("row")
    col = lax.axis_index("col")
    layer = lax.axis_index("layer")
    chip, core = lax.div(row, 2), lax.rem(row, 2)
    partner = {"row": chip * 2 + 1 - core}
    empty = rows * pieces

    def row_at(step):
        return lax.rem(chip + step + chips, chips) * 2 + core

    def col_at(step):
        return lax.rem(col + step + cols, cols)

    def twin_at(step):
        return lax.rem(chip + step + chips, chips) * 2 + 1 - core

    layers = 4
    after = lax.rem(layer + 1, layers)
    before = lax.rem(layer + 3, layers)
    across = lax.rem(layer + 2, layers)

    def send(src, dst, send_sem, recv_sem, where):
        copy = pltpu.make_async_remote_copy(
            src_ref=src, dst_ref=dst, send_sem=send_sem, recv_sem=recv_sem,
            device_id=where, device_id_type=MESH,
        )
        copy.start()
        sent.append(copy)

    def wait_recv(dst, send_sem, recv_sem, where):
        pltpu.make_async_remote_copy(
            src_ref=dst, dst_ref=dst, send_sem=send_sem, recv_sem=recv_sem,
            device_id=where, device_id_type=MESH,
        ).wait_recv()

    sent = []

    lane = lax.broadcasted_iota(jnp.int32, (8, LANES), 1)
    codes = jnp.full((8, LANES), -1, jnp.int32)
    for slot in range(cols):
        codes = jnp.where(lane == slot, a_codes[slot], codes)
    a_tags[col] = codes
    slot_of = lax.broadcasted_iota(jnp.int32, (rows, LANES), 0)
    codes = jnp.full((rows, LANES), -1, jnp.int32)
    for slot in range(rows):
        codes = jnp.where(slot_of == slot, b_codes[slot], codes)
    b_tags[row] = codes
    for stack in b_all:
        stack[empty] = jnp.zeros(stack.shape[1:], stack.dtype)

    local = [pltpu.make_async_copy(a_in, a_all.at[col], here.at[cols])]
    for kind in range(cols):
        local.append(
            pltpu.make_async_copy(
                b_in.at[:, kind], b_all[kind].at[pl.ds(row * pieces, pieces)], here.at[kind]
            )
        )
    for copy in local:
        copy.start()

    barrier = pltpu.get_barrier_semaphore()
    greeted = [
        {"row": row_at(1)}, {"row": row_at(-1)}, partner,
        {"col": col_at(1)}, {"col": col_at(-1)},
        {"layer": after}, {"layer": before},
    ]
    for device in greeted:
        pl.semaphore_signal(barrier, inc=1, device_id=device, device_id_type=MESH)
    pl.semaphore_wait(barrier, len(greeted))

    half_a = cols // 2
    order = [kind for pair in zip(range(half_a), range(half_a, cols)) for kind in pair]

    def ways(kind):
        return 1 if kind < half_a else -1

    def b_place(kind, source):
        return b_all[kind].at[pl.ds(source * pieces, pieces)]

    def b_forward(kind, hop, src):
        source = row_at(-ways(kind) * hop)
        send(
            src, b_place(kind, source), b_send.at[kind, hop], b_recv.at[kind, hop],
            {"row": row_at(ways(kind))},
        )

    def b_share(kind, hop, src):
        source = row_at(-ways(kind) * hop)
        send(src, b_place(kind, source), p_send.at[kind, hop], p_recv.at[kind, hop], partner)

    def b_arrive(kind, hop):
        place = b_place(kind, row_at(-ways(kind) * hop))
        wait_recv(
            place, b_send.at[kind, hop - 1], b_recv.at[kind, hop - 1], {"row": row_at(ways(kind))}
        )
        return place

    def b_shared(kind, hop):
        wait_recv(
            b_place(kind, twin_at(-ways(kind) * hop)),
            p_send.at[kind, hop], p_recv.at[kind, hop], partner,
        )

    def a_place(way, source):
        return a_all.at[source, pl.ds(half_a * way, half_a)]

    def a_forward(way, hop, src):
        step = 1 - 2 * way
        source = col_at(-step * hop)
        send(
            src, a_place(way, source), a_send.at[way, hop], a_recv.at[way, hop],
            {"col": col_at(step)},
        )

    def a_arrive(way, hop):
        step = 1 - 2 * way
        place = a_place(way, col_at(-step * hop))
        wait_recv(place, a_send.at[way, hop - 1], a_recv.at[way, hop - 1], {"col": col_at(step)})
        return place

    def tag_reach(size, way):
        return size // 2 if way == 0 else size - 1 - size // 2

    def at_forward(way, hop):
        step = 1 - 2 * way
        place = a_tags.at[col_at(-step * hop)]
        send(place, place, at_send.at[way, hop], at_recv.at[way, hop], {"col": col_at(step)})

    def bt_forward(way, hop):
        step = 1 - 2 * way
        place = b_tags.at[row_at(-step * hop)]
        send(place, place, bt_send.at[way, hop], bt_recv.at[way, hop], {"row": row_at(step)})

    def bt_share(way, hop):
        place = b_tags.at[row_at(-(1 - 2 * way) * hop)]
        send(place, place, pt_send.at[way, hop], pt_recv.at[way, hop], partner)

    for way in range(2):
        if tag_reach(cols, way) > 0:
            at_forward(way, 0)
        if tag_reach(chips, way) > 0:
            bt_forward(way, 0)
    bt_share(0, 0)
    for index, kind in enumerate(order):
        b_forward(kind, 0, b_in.at[:, kind])
        if index < 2:
            a_forward(index, 0, a_in.at[pl.ds(half_a * index, half_a)])
    for kind in order:
        b_share(kind, 0, b_in.at[:, kind])

    def tags_step(hop):
        for way in range(2):
            step = 1 - 2 * way
            if hop <= tag_reach(cols, way):
                wait_recv(
                    a_tags.at[col_at(-step * hop)], at_send.at[way, hop - 1],
                    at_recv.at[way, hop - 1], {"col": col_at(step)},
                )
                if hop < tag_reach(cols, way):
                    at_forward(way, hop)
            if hop <= tag_reach(chips, way):
                wait_recv(
                    b_tags.at[row_at(-step * hop)], bt_send.at[way, hop - 1],
                    bt_recv.at[way, hop - 1], {"row": row_at(step)},
                )
                if hop < tag_reach(chips, way):
                    bt_forward(way, hop)
                bt_share(way, hop)

    def make_table():
        for way in range(2):
            for hop in range(0 if way == 0 else 1, tag_reach(chips, way) + 1):
                wait_recv(
                    b_tags.at[twin_at(-(1 - 2 * way) * hop)],
                    pt_send.at[way, hop], pt_recv.at[way, hop], partner,
                )
        owner = lax.broadcasted_iota(jnp.int32, (8, LANES), 0)
        tags = jnp.full((8, LANES), -1, jnp.int32)
        for source in range(cols):
            tags = jnp.where(owner == source, a_tags[source], tags)
        one = jnp.ones((8, LANES), jnp.int32)
        zero = jnp.zeros((8, LANES), jnp.int32)
        row_of = zero
        for bound in range(1, RB):
            row_of = row_of + jnp.where(tags >= bound * pieces * KB, one, zero)
        rest = tags - row_of * (pieces * KB)
        part_of = zero
        for bound in range(1, pieces):
            part_of = part_of + jnp.where(rest >= bound * KB, one, zero)
        inner_of = rest - part_of * KB
        piece = lax.rem(lane + row, cols) + cols * part_of
        live = tags >= 0
        first = jnp.where(live, (piece * KB + inner_of) * CB, -1000)
        wanted = [first + column for column in range(CB)]
        piece_b = lax.rem(slot_of + col, rows)

        def scan(source, found):
            tags_b = b_tags[source]
            position = jnp.where(tags_b >= 0, tags_b + piece_b * (KB * CB), -5000)
            found = list(found)
            for slot in range(rows):
                spot = jnp.broadcast_to(position[slot : slot + 1, :], (8, LANES))
                value = source * pieces + slot // cols
                for column in range(CB):
                    found[column] = jnp.where(wanted[column] == spot, value, found[column])
            return tuple(found)

        start = tuple(jnp.full((8, LANES), empty, jnp.int32) for _ in range(CB))
        found = lax.fori_loop(0, rows, scan, start)
        for column in range(CB):
            table[column] = found[column]
        table[CB] = jnp.where(live, row_of, -1)
        copy = pltpu.make_async_copy(table, table_s, table_sem)
        copy.start()
        copy.wait()

    def b_pass(hop):
        for kind in order:
            place = b_arrive(kind, hop)
            b_forward(kind, hop, place)
            b_share(kind, hop, place)

    def a_pass(hop):
        for way in range(2):
            place = a_arrive(way, hop)
            if hop < cols - 1:
                a_forward(way, hop, place)

    table_after = max(tag_reach(cols, 0), tag_reach(chips, 0))
    for hop in range(1, chips - 1):
        b_pass(hop)
        tags_step(hop)
        if hop < cols:
            a_pass(hop)
        if hop == table_after:
            make_table()
    for hop in range(max(chips - 1, 1), table_after + 1):
        tags_step(hop)
    if table_after >= chips - 1:
        make_table()
    for hop in range(max(chips - 1, 1), cols):
        a_pass(hop)

    def multiply(kind, is_first):
        local[1 + kind].wait()
        for hop in range(chips):
            b_shared(kind, hop)
        slot = lax.rem(kind + col + rows - row, cols)
        for source in range(cols):
            block = a_all[source, slot]
            home = table_s[CB, source, slot]
            across_k = pl.ds(source * LANES, LANES)
            for target in range(RB):
                left[pl.ds(target * LANES, LANES), across_k] = jnp.where(
                    home == target, block, jnp.zeros_like(block)
                )
            for column in range(CB):
                right[across_k, pl.ds(column * LANES, LANES)] = b_all[kind][
                    table_s[column, source, slot]
                ]
        wide = CB * LANES // 2
        for half in range(2):
            product = jnp.dot(
                left[...], right[:, pl.ds(half * wide, wide)], preferred_element_type=jnp.float32
            ).reshape(RB, LANES, wide)
            if is_first:
                total[:, half] = product
            else:
                total[:, half] = total[:, half] + product

    local[0].wait()
    pairs = [order[i : i + 2] for i in range(0, cols, 2)]
    for index, pair in enumerate(pairs + [None]):
        if pair is not None:
            for kind in pair:
                b_share(kind, chips - 1, b_arrive(kind, chips - 1))
        if index > 0:
            for kind in pairs[index - 1]:
                multiply(kind, kind == order[0])

    to_after, to_before = {"layer": after}, {"layer": before}

    def x_send_to(index, src, dst, where):
        send(src, dst, x_send.at[index], x_recv.at[index], where)

    x_send_to(0, total.at[across, 0], passing.at[0], to_after)
    x_send_to(1, total.at[across, 1], passing.at[1], to_before)
    x_send_to(2, total.at[after, 1], arrived.at[0, 1], to_after)
    x_send_to(3, total.at[before, 0], arrived.at[1, 0], to_before)
    wait_recv(passing.at[0], x_send.at[0], x_recv.at[0], to_after)
    total[after, 0] = total[after, 0] + passing[0]
    x_send_to(4, total.at[after, 0], arrived.at[0, 0], to_after)
    wait_recv(passing.at[1], x_send.at[1], x_recv.at[1], to_before)
    total[before, 1] = total[before, 1] + passing[1]
    x_send_to(5, total.at[before, 1], arrived.at[1, 1], to_before)
    wait_recv(arrived.at[0, 1], x_send.at[2], x_recv.at[2], to_after)
    wait_recv(arrived.at[1, 0], x_send.at[3], x_recv.at[3], to_before)
    wait_recv(arrived.at[0, 0], x_send.at[4], x_recv.at[4], to_after)
    wait_recv(arrived.at[1, 1], x_send.at[5], x_recv.at[5], to_before)
    wide = CB * LANES // 2
    for half in range(2):
        out[:, pl.ds(half * wide, wide)] = (
            total[layer, half] + arrived[0, half] + arrived[1, half]
        ).astype(out.dtype)
    for copy in sent:
        copy.wait_send()


def shards(a_blocks, a_codes, b_blocks, b_codes):
    rows = lax.axis_size("row")
    cols = lax.axis_size("col")
    pieces = rows // cols
    chips = rows // 2
    size = a_blocks.shape[1]
    b_blocks = b_blocks.reshape(pieces, cols, size, size)
    anywhere = pl.BlockSpec(memory_space=pl.ANY)
    scalars = pl.BlockSpec(memory_space=pltpu.SMEM)
    dma = pltpu.SemaphoreType.DMA
    wide = CB * size // 2
    scratch = [
        pltpu.VMEM((cols, cols, size, size), jnp.bfloat16),
        pltpu.VMEM((cols, 8, LANES), jnp.int32),
        pltpu.VMEM((rows, rows, LANES), jnp.int32),
        pltpu.VMEM((CB + 1, 8, LANES), jnp.int32),
        pltpu.SMEM((CB + 1, 8, LANES), jnp.int32),
        pltpu.VMEM((RB * size, cols * size), jnp.bfloat16),
        pltpu.VMEM((cols * size, CB * size), jnp.bfloat16),
        pltpu.VMEM((RB, 2, size, wide), jnp.float32),
        pltpu.VMEM((2, size, wide), jnp.float32),
        pltpu.VMEM((2, 2, size, wide), jnp.float32),
        dma((2, cols)), dma((2, cols)), dma((2, cols)), dma((2, cols)),
        dma((cols, chips)), dma((cols, chips)), dma((cols, chips)), dma((cols, chips)),
        dma((2, chips)), dma((2, chips)), dma((2, chips)), dma((2, chips)),
        dma((cols + 1,)), dma(()), dma((6,)), dma((6,)),
    ] + [pltpu.VMEM((rows * pieces + 1, size, size), jnp.bfloat16)] * cols
    return pl.pallas_call(
        functools.partial(kernel, rows, cols, pieces),
        out_shape=jax.ShapeDtypeStruct((size, CB * size), jnp.bfloat16),
        in_specs=[scalars, scalars, anywhere, anywhere],
        out_specs=pl.BlockSpec(memory_space=pltpu.VMEM),
        scratch_shapes=scratch,
        compiler_params=pltpu.CompilerParams(
            collective_id=0, has_side_effects=True, vmem_limit_bytes=32 * 1024 * 1024
        ),
        name="gather_multiply_scatter",
    )(a_codes, b_codes, a_blocks, b_blocks)


def solution(mesh):
    placed = (
        P(("row", "col", "layer"), None, None),
        P(("row", "col", "layer")),
        P(("row", "col", "layer"), None, None),
        P(("row", "col", "layer")),
    )
    return jax.shard_map(
        shards, mesh=mesh, in_specs=placed, out_specs=P(("row", "layer"), "col"), check_vma=False
    )
```

time: 349 us -> 81.3 us (0.23)
  starting transfers between devices: 178 us -> 0 us
  Pallas kernels: 0 us -> 77.8 us
  waiting for transfers between devices: 75.2 us -> 0 us
  blocking collectives: 33.6 us -> 0 us
  matrix products: 24.6 us -> 0 us
  between operations: 13.5 us -> 0.01 us
  local copies, waits for them, and re-layouts: 14.8 us -> 3.32 us
  other arithmetic: 3.58 us -> 0 us
    ppermute x60 -> x0, starting transfers between devices: 165 us -> none  [from_behind(): return lax.ppermute(block, axis, route)]
    pallas_call x0 -> x1, Pallas kernels: none -> 77.8 us  [shards(): pl.pallas_call(functools.partial(kernel, rows, cols, pieces), out_shape=j...]
    all_to_all x2 -> x0, blocking collectives: 33.6 us -> none  [the longest x1 19.2 us: shards(): lax.all_to_all(b_codes, 'row', split_axis=0, concat_axis=0, tiled=True)]
    reduce_scatter x1 -> x0, waiting for transfers between devices: 29.2 us -> none  [shards(): lax.psum_scatter(accumulated, 'layer', scatter_dimension=0, tiled=True)]
    dot_general x48 -> x0, matrix products: 24.6 us -> none  [the longest x16 13.2 us: multiply(): jnp.dot(left_tile, right_tile, preferred_element_type=jnp.float32)]
    ppermute x60 -> x0, waiting for transfers between devices: 23.9 us -> none  [from_behind(): return lax.ppermute(block, axis, route)]
    all_to_all x2 -> x0, waiting for transfers between devices: 22.2 us -> none  [the longest x1 16.5 us: shards(): lax.all_to_all(b_blocks, 'row', split_axis=0, concat_axis=0, tiled=True)]
    all_to_all x2 -> x0, starting transfers between devices: 12.8 us -> none  [the longest x1 7.65 us: shards(): lax.all_to_all(a_codes, 'col', split_axis=0, concat_axis=0, tiled=True)]
  transfers between devices with their start and end apart: 63 -> 0, of which waited for: 11 -> 0; matrix products, arithmetic and copies ran while one was open for 10% -> 0% of each run, Pallas kernels for 0% -> 0%
where the time goes in v1:
time: 81.3 us; the launch traced here: 81.1 us
  Pallas kernels  77.8 us (96%)
  local copies, waits for them, and re-layouts  3.32 us (4%)
    pallas_call x1, Pallas kernels, shards(): pl.pallas_call(functools.partial(kernel, rows, cols, pieces), out_shape=j...  77.8 us
    unnamed x9, local copies, waits for them, and re-layouts  3.32 us

profile of v1, /device:TPU:1, one launch (start us, length us, event | category | flops | bytes accessed | tf_op | source)
XLA Modules:
  0.0 81.1 jit_solution(17222064166055137412)
XLA Ops:
  0.0 0.0 copy-start.3
  0.0 0.0 copy-start.2
  0.0 0.7 copy-done.3
  0.7 0.0 copy-done.2
  0.7 0.0 copy-start
  0.7 1.0 %copy-done = bf16[16,128,128]{2,1,0:T(8,128)(2,1)S(1)} copy-done((bf16[16,128,128]{2,1,0:T(8,128)(2,1)S(1)}, bf16[16,128,128]{2,1,0:T(8,128)(2,1)}, u32[]{:S(2)}) %copy-start) | copy-done | bytes 524312
  1.7 0.0 copy-start.1
  1.7 0.9 %copy-done.1 = bf16[8,128,128]{2,1,0:T(8,128)(2,1)S(1)} copy-done((bf16[8,128,128]{2,1,0:T(8,128)(2,1)S(1)}, bf16[8,128,128]{2,1,0:T(8,128)(2,1)}, u32[]{:S(2)}) %copy-start.1) | copy-done | bytes 262168
  2.7 77.8 %gather_multiply_scatter.1 = bf16[128,512]{1,0:T(8,128)(2,1)S(1)} custom-call(s32[8]{0:T(128)S(1)} %copy-done.2, s32[16]{0:T(128)S(1)} %copy-done.3, bf16[8,128,128]{2,1,0:T(8,128)(2,1)S(1)} %copy-done.1, bf16[2,8,128,128]{3,2,1,0:T(8,128)(2,1)S(1)} %bitcast.1), custom_call_target="tpu_custom_call" | custom-call | tf_op jit(solution)/shard_map/gather_multiply_scatter/pallas_call | solution.py:361
  80.5 0.7 copy.6
Async XLA Ops:
  0.0 0.7 copy-start.3
  0.0 0.7 copy-start.2
  0.7 1.0 %copy-start = (bf16[16,128,128]{2,1,0:T(8,128)(2,1)S(1)}, bf16[16,128,128]{2,1,0:T(8,128)(2,1)}, u32[]{:S(2)}) copy-start(bf16[16,128,128]{2,1,0:T(8,128)(2,1)} %param.6) | copy-start | bytes 1572868
  1.7 0.9 %copy-start.1 = (bf16[8,128,128]{2,1,0:T(8,128)(2,1)S(1)}, bf16[8,128,128]{2,1,0:T(8,128)(2,1)}, u32[]{:S(2)}) copy-start(bf16[8,128,128]{2,1,0:T(8,128)(2,1)} %a_in.1) | copy-start | bytes 786436

commit v2 on v1

--- a/solution.py
+++ b/solution.py
@@ -239,93 +239,132 @@
         copy.start()
         copy.wait()
 
-    def b_pass(hop):
-        for kind in order:
-            place = b_arrive(kind, hop)
-            b_forward(kind, hop, place)
-            b_share(kind, hop, place)
-
     def a_pass(hop):
         for way in range(2):
             place = a_arrive(way, hop)
             if hop < cols - 1:
                 a_forward(way, hop, place)
 
-    table_after = max(tag_reach(cols, 0), tag_reach(chips, 0))
-    for hop in range(1, chips - 1):
-        b_pass(hop)
-        tags_step(hop)
-        if hop < cols:
-            a_pass(hop)
-        if hop == table_after:
-            make_table()
-    for hop in range(max(chips - 1, 1), table_after + 1):
-        tags_step(hop)
-    if table_after >= chips - 1:
-        make_table()
-    for hop in range(max(chips - 1, 1), cols):
-        a_pass(hop)
-
-    def multiply(kind, is_first):
+    homes = [across, after, before, layer]
+
+    def slot_for(kind):
+        return lax.rem(kind + col + rows - row, cols)
+
+    def place_left(kind):
+        slot = slot_for(kind)
+        for source in range(cols):
+            block = a_all[source, slot]
+            home = table_s[CB, source, slot]
+            for target in range(RB):
+                left[kind, pl.ds(target * LANES, LANES), pl.ds(source * LANES, LANES)] = (
+                    jnp.where(home == homes[target], block, jnp.zeros_like(block))
+                )
+
+    def place_right(kind, index):
         local[1 + kind].wait()
         for hop in range(chips):
             b_shared(kind, hop)
-        slot = lax.rem(kind + col + rows - row, cols)
+        slot = slot_for(kind)
         for source in range(cols):
-            block = a_all[source, slot]
-            home = table_s[CB, source, slot]
-            across_k = pl.ds(source * LANES, LANES)
-            for target in range(RB):
-                left[pl.ds(target * LANES, LANES), across_k] = jnp.where(
-                    home == target, block, jnp.zeros_like(block)
-                )
             for column in range(CB):
-                right[across_k, pl.ds(column * LANES, LANES)] = b_all[kind][
-                    table_s[column, source, slot]
-                ]
-        wide = CB * LANES // 2
+                right[index, pl.ds(source * LANES, LANES), pl.ds(column * LANES, LANES)] = (
+                    b_all[kind][table_s[column, source, slot]]
+                )
+
+    wide = CB * LANES // 2
+
+    def multiply(kinds, first_row, row_count, is_first):
         for half in range(2):
-            product = jnp.dot(
-                left[...], right[:, pl.ds(half * wide, wide)], preferred_element_type=jnp.float32
-            ).reshape(RB, LANES, wide)
-            if is_first:
-                total[:, half] = product
-            else:
-                total[:, half] = total[:, half] + product
-
-    local[0].wait()
+            product = None
+            for index, kind in enumerate(kinds):
+                term = jnp.dot(
+                    left[kind, pl.ds(first_row * LANES, row_count * LANES), :],
+                    right[index, :, pl.ds(half * wide, wide)],
+                    preferred_element_type=jnp.float32,
+                )
+                product = term if product is None else product + term
+            product = product.reshape(row_count, LANES, wide)
+            part = pl.ds(first_row, row_count)
+            total[part, half] = product if is_first else total[part, half] + product
+
+    table_after = max(tag_reach(cols, 0), tag_reach(chips, 0))
+    progress = {"a": 1, "table": False, "left": 0}
+
+    def a_until(event):
+        while progress["a"] < cols and event >= 7 * progress["a"] - 5:
+            a_pass(progress["a"])
+            progress["a"] += 1
+            if progress["a"] == cols:
+                local[0].wait()
+
+    def one_left():
+        if progress["a"] == cols and progress["table"] and progress["left"] < cols:
+            place_left(order[progress["left"]])
+            progress["left"] += 1
+
+    for hop in range(1, chips - 1):
+        for index, kind in enumerate(order):
+            place = b_arrive(kind, hop)
+            b_forward(kind, hop, place)
+            b_share(kind, hop, place)
+            a_until((hop - 1) * cols + index)
+            one_left()
+        tags_step(hop)
+        if hop == table_after:
+            make_table()
+            progress["table"] = True
+    for hop in range(max(chips - 1, 1), table_after + 1):
+        tags_step(hop)
+    if not progress["table"]:
+        make_table()
+        progress["table"] = True
+    a_until(7 * cols)
+
     pairs = [order[i : i + 2] for i in range(0, cols, 2)]
-    for index, pair in enumerate(pairs + [None]):
-        if pair is not None:
-            for kind in pair:
-                b_share(kind, chips - 1, b_arrive(kind, chips - 1))
-        if index > 0:
-            for kind in pairs[index - 1]:
-                multiply(kind, kind == order[0])
+    early = pairs[: max(len(pairs) - 2, 0)]
+    late = [kind for pair in pairs[len(early) :] for kind in pair]
+
+    def finish(pair):
+        for kind in pair:
+            b_share(kind, chips - 1, b_arrive(kind, chips - 1))
+            one_left()
+
+    finish(pairs[0])
+    for index, pair in enumerate(pairs):
+        if index + 1 < len(pairs):
+            finish(pairs[index + 1])
+        if pair in early:
+            for part, kind in enumerate(pair):
+                place_right(kind, part)
+            multiply(pair, 0, RB, index == 0)
+    for index, kind in enumerate(late):
+        place_right(kind, index)
 
     to_after, to_before = {"layer": after}, {"layer": before}
 
     def x_send_to(index, src, dst, where):
         send(src, dst, x_send.at[index], x_recv.at[index], where)
 
-    x_send_to(0, total.at[across, 0], passing.at[0], to_after)
-    x_send_to(1, total.at[across, 1], passing.at[1], to_before)
-    x_send_to(2, total.at[after, 1], arrived.at[0, 1], to_after)
-    x_send_to(3, total.at[before, 0], arrived.at[1, 0], to_before)
+    multiply(late, 0, 1, not early)
+    x_send_to(0, total.at[0, 0], passing.at[0], to_after)
+    x_send_to(1, total.at[0, 1], passing.at[1], to_before)
+    multiply(late, 1, 2, not early)
+    x_send_to(2, total.at[1, 1], arrived.at[0, 1], to_after)
+    x_send_to(3, total.at[2, 0], arrived.at[1, 0], to_before)
+    multiply(late, 3, 1, not early)
     wait_recv(passing.at[0], x_send.at[0], x_recv.at[0], to_after)
-    total[after, 0] = total[after, 0] + passing[0]
-    x_send_to(4, total.at[after, 0], arrived.at[0, 0], to_after)
+    total[1, 0] = total[1, 0] + passing[0]
+    x_send_to(4, total.at[1, 0], arrived.at[0, 0], to_after)
     wait_recv(passing.at[1], x_send.at[1], x_recv.at[1], to_before)
-    total[before, 1] = total[before, 1] + passing[1]
-    x_send_to(5, total.at[before, 1], arrived.at[1, 1], to_before)
+    total[2, 1] = total[2, 1] + passing[1]
+    x_send_to(5, total.at[2, 1], arrived.at[1, 1], to_before)
     wait_recv(arrived.at[0, 1], x_send.at[2], x_recv.at[2], to_after)
     wait_recv(arrived.at[1, 0], x_send.at[3], x_recv.at[3], to_before)
     wait_recv(arrived.at[0, 0], x_send.at[4], x_recv.at[4], to_after)
     wait_recv(arrived.at[1, 1], x_send.at[5], x_recv.at[5], to_before)
-    wide = CB * LANES // 2
     for half in range(2):
         out[:, pl.ds(half * wide, wide)] = (
-            total[layer, half] + arrived[0, half] + arrived[1, half]
+            total[3, half] + arrived[0, half] + arrived[1, half]
         ).astype(out.dtype)
     for copy in sent:
         copy.wait_send()
@@ -348,8 +387,8 @@
         pltpu.VMEM((rows, rows, LANES), jnp.int32),
         pltpu.VMEM((CB + 1, 8, LANES), jnp.int32),
         pltpu.SMEM((CB + 1, 8, LANES), jnp.int32),
-        pltpu.VMEM((RB * size, cols * size), jnp.bfloat16),
-        pltpu.VMEM((cols * size, CB * size), jnp.bfloat16),
+        pltpu.VMEM((cols, RB * size, cols * size), jnp.bfloat16),
+        pltpu.VMEM((4, cols * size, CB * size), jnp.bfloat16),
         pltpu.VMEM((RB, 2, size, wide), jnp.float32),
         pltpu.VMEM((2, size, wide), jnp.float32),
         pltpu.VMEM((2, 2, size, wide), jnp.float32),
@@ -365,7 +404,7 @@
         out_specs=pl.BlockSpec(memory_space=pltpu.VMEM),
         scratch_shapes=scratch,
         compiler_params=pltpu.CompilerParams(
-            collective_id=0, has_side_effects=True, vmem_limit_bytes=32 * 1024 * 1024
+            collective_id=0, has_side_effects=True, vmem_limit_bytes=62 * 1024 * 1024
         ),
         name="gather_multiply_scatter",
     )(a_codes, b_codes, a_blocks, b_blocks)

time: 81.3 us -> 77.4 us (0.952)
  Pallas kernels: 77.8 us -> 75.7 us
  local copies, waits for them, and re-layouts: 3.32 us -> 1.57 us
    pallas_call x1, Pallas kernels: 77.8 us -> 75.7 us  [shards(): pl.pallas_call(functools.partial(kernel, rows, cols, pieces), out_shape=j...]
    unnamed x9 -> x1, local copies, waits for them, and re-layouts: 3.32 us -> 1.57 us
where the time goes in v2:
time: 77.4 us; the launch traced here: 77.3 us
  Pallas kernels  75.7 us (98%)
  local copies, waits for them, and re-layouts  1.57 us (2%)
    pallas_call x1, Pallas kernels, shards(): pl.pallas_call(functools.partial(kernel, rows, cols, pieces), out_shape=j...  75.7 us
    unnamed x1, local copies, waits for them, and re-layouts  1.57 us

profile of v2, /device:TPU:1, one launch (start us, length us, event | category | flops | bytes accessed | tf_op | source)
XLA Modules:
  0.0 77.3 jit_solution(15058213544294550821)
XLA Ops:
  0.0 75.7 %gather_multiply_scatter.1 = bf16[128,512]{1,0:T(8,128)(2,1)} custom-call(s32[8]{0:T(128)} %a_codes.1, s32[16]{0:T(128)} %b_codes.1, bf16[8,128,128]{2,1,0:T(8,128)(2,1)} %a_in.1, bf16[2,8,128,128]{3,2,1,0:T(8,128)(2,1)} %bitcast.1), custom_call_target="tpu_custom_call" | custom-call | tf_op jit(solution)/shard_map/gather_multiply_scatter/pallas_call | solution.py:400
  75.7 1.6 %copy.6 = bf16[128,512]{1,0:T(8,128)(2,1)} copy(bf16[128,512]{1,0:T(8,128)(2,1)} %gather_multiply_scatter.1) | data formatting | bytes 262144

commit v3 on v2

--- a/solution.py
+++ b/solution.py
@@ -160,16 +160,17 @@
         place = b_tags.at[row_at(-(1 - 2 * way) * hop)]
         send(place, place, pt_send.at[way, hop], pt_recv.at[way, hop], partner)
 
-    for way in range(2):
-        if tag_reach(cols, way) > 0:
-            at_forward(way, 0)
-        if tag_reach(chips, way) > 0:
-            bt_forward(way, 0)
-    bt_share(0, 0)
     for index, kind in enumerate(order):
         b_forward(kind, 0, b_in.at[:, kind])
-        if index < 2:
-            a_forward(index, 0, a_in.at[pl.ds(half_a * index, half_a)])
+        if index == 1:
+            for way in range(2):
+                if tag_reach(cols, way) > 0:
+                    at_forward(way, 0)
+                if tag_reach(chips, way) > 0:
+                    bt_forward(way, 0)
+            bt_share(0, 0)
+            for way in range(2):
+                a_forward(way, 0, a_in.at[pl.ds(half_a * way, half_a)])
     for kind in order:
         b_share(kind, 0, b_in.at[:, kind])
 
@@ -321,7 +322,7 @@
     a_until(7 * cols)
 
     pairs = [order[i : i + 2] for i in range(0, cols, 2)]
-    early = pairs[: max(len(pairs) - 2, 0)]
+    early = pairs[: max(len(pairs) - 1, 0)]
     late = [kind for pair in pairs[len(early) :] for kind in pair]
 
     def finish(pair):
@@ -358,6 +359,8 @@
     wait_recv(passing.at[1], x_send.at[1], x_recv.at[1], to_before)
     total[2, 1] = total[2, 1] + passing[1]
     x_send_to(5, total.at[2, 1], arrived.at[1, 1], to_before)
+    for copy in sent:
+        copy.wait_send()
     wait_recv(arrived.at[0, 1], x_send.at[2], x_recv.at[2], to_after)
     wait_recv(arrived.at[1, 0], x_send.at[3], x_recv.at[3], to_before)
     wait_recv(arrived.at[0, 0], x_send.at[4], x_recv.at[4], to_after)
@@ -366,8 +369,6 @@
         out[:, pl.ds(half * wide, wide)] = (
             total[3, half] + arrived[0, half] + arrived[1, half]
         ).astype(out.dtype)
-    for copy in sent:
-        copy.wait_send()
 
 
 def shards(a_blocks, a_codes, b_blocks, b_codes):

time: 77.4 us -> 76.3 us (0.986)
  Pallas kernels: 75.7 us -> 74.5 us
    pallas_call x1, Pallas kernels: 75.7 us -> 74.5 us  [shards(): pl.pallas_call(functools.partial(kernel, rows, cols, pieces), out_shape=j...]
where the time goes in v3:
time: 76.3 us; the launch traced here: 76.1 us
  Pallas kernels  74.5 us (98%)
  local copies, waits for them, and re-layouts  1.57 us (2%)
    pallas_call x1, Pallas kernels, shards(): pl.pallas_call(functools.partial(kernel, rows, cols, pieces), out_shape=j...  74.5 us
    unnamed x1, local copies, waits for them, and re-layouts  1.57 us

profile of v3, /device:TPU:1, one launch (start us, length us, event | category | flops | bytes accessed | tf_op | source)
XLA Modules:
  0.0 76.1 jit_solution(12751396295427464431)
XLA Ops:
  0.0 74.5 %gather_multiply_scatter.1 = bf16[128,512]{1,0:T(8,128)(2,1)} custom-call(s32[8]{0:T(128)} %a_codes.1, s32[16]{0:T(128)} %b_codes.1, bf16[8,128,128]{2,1,0:T(8,128)(2,1)} %a_in.1, bf16[2,8,128,128]{3,2,1,0:T(8,128)(2,1)} %bitcast.1), custom_call_target="tpu_custom_call" | custom-call | tf_op jit(solution)/shard_map/gather_multiply_scatter/pallas_call | solution.py:401
  74.6 1.6 %copy.6 = bf16[128,512]{1,0:T(8,128)(2,1)} copy(bf16[128,512]{1,0:T(8,128)(2,1)} %gather_multiply_scatter.1) | data formatting | bytes 262144

commit v4 on v3

--- a/solution.py
+++ b/solution.py
@@ -252,12 +252,13 @@
         return lax.rem(kind + col + rows - row, cols)
 
     def place_left(kind):
+        pair, at = order.index(kind) // 2, order.index(kind) % 2 * cols * LANES
         slot = slot_for(kind)
         for source in range(cols):
             block = a_all[source, slot]
             home = table_s[CB, source, slot]
             for target in range(RB):
-                left[kind, pl.ds(target * LANES, LANES), pl.ds(source * LANES, LANES)] = (
+                left[pair, pl.ds(target * LANES, LANES), pl.ds(at + source * LANES, LANES)] = (
                     jnp.where(home == homes[target], block, jnp.zeros_like(block))
                 )
 
@@ -268,7 +269,7 @@
         slot = slot_for(kind)
         for source in range(cols):
             for column in range(CB):
-                right[index, pl.ds(source * LANES, LANES), pl.ds(column * LANES, LANES)] = (
+                right[pl.ds((index * cols + source) * LANES, LANES), pl.ds(column * LANES, LANES)] = (
                     b_all[kind][table_s[column, source, slot]]
                 )
 
@@ -276,15 +277,11 @@
 
     def multiply(kinds, first_row, row_count, is_first):
         for half in range(2):
-            product = None
-            for index, kind in enumerate(kinds):
-                term = jnp.dot(
-                    left[kind, pl.ds(first_row * LANES, row_count * LANES), :],
-                    right[index, :, pl.ds(half * wide, wide)],
-                    preferred_element_type=jnp.float32,
-                )
-                product = term if product is None else product + term
-            product = product.reshape(row_count, LANES, wide)
+            product = jnp.dot(
+                left[order.index(kinds[0]) // 2, pl.ds(first_row * LANES, row_count * LANES), :],
+                right[:, pl.ds(half * wide, wide)],
+                preferred_element_type=jnp.float32,
+            ).reshape(row_count, LANES, wide)
             part = pl.ds(first_row, row_count)
             total[part, half] = product if is_first else total[part, half] + product
 
@@ -388,8 +385,8 @@
         pltpu.VMEM((rows, rows, LANES), jnp.int32),
         pltpu.VMEM((CB + 1, 8, LANES), jnp.int32),
         pltpu.SMEM((CB + 1, 8, LANES), jnp.int32),
-        pltpu.VMEM((cols, RB * size, cols * size), jnp.bfloat16),
-        pltpu.VMEM((4, cols * size, CB * size), jnp.bfloat16),
+        pltpu.VMEM((cols // 2, RB * size, 2 * cols * size), jnp.bfloat16),
+        pltpu.VMEM((2 * cols * size, CB * size), jnp.bfloat16),
         pltpu.VMEM((RB, 2, size, wide), jnp.float32),
         pltpu.VMEM((2, size, wide), jnp.float32),
         pltpu.VMEM((2, 2, size, wide), jnp.float32),

time: 76.3 us -> 76.2 us (level)
  no operation moved by 1% of the time
where the time goes in v4:
time: 76.2 us; the launch traced here: 76 us
  Pallas kernels  74.5 us (98%)
  local copies, waits for them, and re-layouts  1.57 us (2%)
    pallas_call x1, Pallas kernels, shards(): pl.pallas_call(functools.partial(kernel, rows, cols, pieces), out_shape=j...  74.5 us
    unnamed x1, local copies, waits for them, and re-layouts  1.57 us

profile of v4, /device:TPU:1, one launch (start us, length us, event | category | flops | bytes accessed | tf_op | source)
XLA Modules:
  0.0 76.0 jit_solution(6495185482517444291)
XLA Ops:
  0.0 74.5 %gather_multiply_scatter.1 = bf16[128,512]{1,0:T(8,128)(2,1)} custom-call(s32[8]{0:T(128)} %a_codes.1, s32[16]{0:T(128)} %b_codes.1, bf16[8,128,128]{2,1,0:T(8,128)(2,1)} %a_in.1, bf16[2,8,128,128]{3,2,1,0:T(8,128)(2,1)} %bitcast.1), custom_call_target="tpu_custom_call" | custom-call | tf_op jit(solution)/shard_map/gather_multiply_scatter/pallas_call | solution.py:398
  74.5 1.6 %copy.6 = bf16[128,512]{1,0:T(8,128)(2,1)} copy(bf16[128,512]{1,0:T(8,128)(2,1)} %gather_multiply_scatter.1) | data formatting | bytes 262144
